TPU v7x, 32 devices: a whole 2x2x4 slice. The times are simulated.
32 devices in a mesh: rhombus: 4 (over z), tile: 8 (over y, x, core).
Axes of the slice: x: 2, y: 2, z: 4, core: 2. Of those that a mesh axis runs over, the one named last changes fastest.
Arguments:
- fine_latent: bfloat16 [16384, 512], P(('rhombus', 'tile')), may hold values from -6 to 6
- mid_latent: bfloat16 [1024, 512], P(('rhombus', 'tile')), may hold values from -6 to 6
- coarse_latent: bfloat16 [642, 512], replicated, may hold values from -6 to 6
- fine_parent: int32 [16384], P(('rhombus', 'tile')), may hold values from 0 to 95, as said below
- mid_parent: int32 [1024], P(('rhombus', 'tile')), may hold values from 0 to 641
- halo_rows: int32 [8192], P(('rhombus', 'tile')), may hold values from 0 to 511
- edge_source: int32 [98304], P(('rhombus', 'tile')), may hold values from 0 to 767
- edge_target: int32 [98304], P(('rhombus', 'tile')), may hold values from 0 to 512, as said below
- w_child: bfloat16 [512, 512], replicated, may hold values from -1 to 1
- mid_w1: bfloat16 [512, 512], replicated, may hold values from -0.25 to 0.25
- mid_w2: bfloat16 [512, 512], replicated, may hold values from -0.5 to 0.5
- mid_w3: bfloat16 [512, 512], replicated, may hold values from -0.25 to 0.25
- w_coarse: bfloat16 [512, 512], replicated, may hold values from -1 to 1
- coarse_w1: bfloat16 [512, 512], replicated, may hold values from -0.25 to 0.25
- coarse_w2: bfloat16 [512, 512], replicated, may hold values from -0.5 to 0.5
- coarse_w3: bfloat16 [512, 512], replicated, may hold values from -0.25 to 0.25
- w_descend: bfloat16 [512, 512], replicated, may hold values from -0.25 to 0.25
- w_fine: bfloat16 [512, 512], replicated, may hold values from -0.25 to 0.25
- edge_w_src: bfloat16 [512, 512], replicated, may hold values from -1 to 1
- edge_w_dst: bfloat16 [512, 512], replicated, may hold values from -0.25 to 0.25
- edge_w2: bfloat16 [512, 512], replicated, may hold values from -0.25 to 0.25
- node_w1: bfloat16 [512, 512], replicated, may hold values from -0.25 to 0.25
- node_w2: bfloat16 [512, 512], replicated, may hold values from -0.125 to 0.125
- node_w3: bfloat16 [512, 512], replicated, may hold values from -0.25 to 0.25
Outputs:
- fine_out: bfloat16 [16384, 512], P(('rhombus', 'tile'))
- mid_out: bfloat16 [1024, 512], P(('rhombus', 'tile'))
- coarse_out: bfloat16 [642, 512], replicated
Inputs may be any that keep to these rules, and one draw needn't show every extreme that they name: `fine_parent`: in tile t of a group, an entry p < 32 names a middle slot of the same tile, 32 <= p < 64 a slot of tile t - 1, 64 <= p a slot of tile t + 1; tile 0 never names the tile before and the last tile of a group never names the tile after. `edge_target`: in each tile the live slots come first and name a fine row of that tile; the remaining slots hold 512. Each tile has at least 1536 live slots, and some tile has all 3072 slots live.
All inputs are finite; a program needn't handle non-finite values.
Results may differ from a plain program's by a relative error of at most 0.013.
Values may be sent and summed in bfloat16 or wider, within the bound.
A program may use at most 64 MiB of HBM per device.

v0:
```python
import jax
import jax.numpy as jnp
from jax import lax
from jax.sharding import PartitionSpec as P

EPSILON = 1e-05


def extended_2(shard, sides, width):
    for axis, dim in sides:
        size, length = (lax.axis_size(axis), shard.shape[dim])
        up = [(i, (i + 1) % size) for i in range(size - 1)]
        down = [(j, i) for i, j in up]
        last = lax.slice_in_dim(shard, length - width, length, axis=dim)
        leading = lax.slice_in_dim(shard, 0, width, axis=dim)
        before = lax.ppermute(last, axis, up)
        after = lax.ppermute(leading, axis, down)
        shard = jnp.concatenate([before, shard, after], axis=dim)
    return shard


def product(left, right):
    return jnp.dot(left, right, preferred_element_type=jnp.float32)


def normed(values):
    return values / jnp.sqrt(jnp.mean(values * values, axis=-1, keepdims=True) + EPSILON)


def node_update(latent, incoming, first, second, third):
    hidden = jax.nn.silu(product(latent, first) + product(incoming, second)).astype(jnp.bfloat16)
    return (latent.astype(jnp.float32) + normed(product(hidden, third))).astype(jnp.bfloat16)


def coarse_update(latent, incoming, coarse_w1, coarse_w2, coarse_w3, w_descend):
    updated = node_update(latent, incoming.astype(jnp.bfloat16), coarse_w1, coarse_w2, coarse_w3)
    return (updated, product(updated, w_descend).astype(jnp.bfloat16))


def selector_rows(row_ids, width):
    columns = lax.broadcasted_iota(jnp.int32, (row_ids.shape[0], width), 1)
    return (columns == row_ids[:, None]).astype(jnp.bfloat16)


def edge_update(
    node_table, lifted, source, target, edge_w_src, edge_w_dst, edge_w2, node_w1, node_w2, node_w3
):
    fine_count = lifted.shape[0]
    sender = product(node_table, edge_w_src).astype(jnp.bfloat16)
    receiver = product(lifted, edge_w_dst).astype(jnp.bfloat16)
    source_pick = selector_rows(source, node_table.shape[0])
    target_pick = selector_rows(target, fine_count)
    edge_sum = product(source_pick, sender) + product(target_pick, receiver)
    edge_hidden = jax.nn.silu(edge_sum).astype(jnp.bfloat16)
    hidden_sums = lax.dot_general(
        target_pick, edge_hidden, (((0,), (0,)), ((), ())), preferred_element_type=jnp.float32
    )
    aggregate = jnp.dot(hidden_sums, edge_w2.astype(jnp.float32), precision=lax.Precision.HIGHEST)
    return node_update(lifted, aggregate.astype(jnp.bfloat16), node_w1, node_w2, node_w3)


def on_device(
    fine_latent,
    mid_latent,
    coarse_latent,
    fine_parent,
    mid_parent,
    halo_rows,
    edge_source,
    edge_target,
    w_child,
    mid_w1,
    mid_w2,
    mid_w3,
    w_coarse,
    coarse_w1,
    coarse_w2,
    coarse_w3,
    w_descend,
    w_fine,
    edge_w_src,
    edge_w_dst,
    edge_w2,
    node_w1,
    node_w2,
    node_w3,
):
    fine_count = fine_latent.shape[0]
    mid_count = mid_latent.shape[0]
    coarse_count = coarse_latent.shape[0]
    rim_count = halo_rows.shape[0] // 2
    child_msg = product(fine_latent, w_child).astype(jnp.bfloat16)
    slot_ids = lax.broadcasted_iota(jnp.int32, (3 * mid_count, fine_count), 0)
    picker = (slot_ids == fine_parent[None, :]).astype(jnp.bfloat16)
    partial_sums = product(picker, child_msg)
    extended = extended_2(partial_sums[mid_count:], (("tile", 0),), mid_count)
    mid_in = partial_sums[:mid_count] + extended[:mid_count] + extended[3 * mid_count :]
    mid_up = node_update(mid_latent, mid_in.astype(jnp.bfloat16), mid_w1, mid_w2, mid_w3)
    mid_msg = product(mid_up, w_coarse).astype(jnp.bfloat16)
    coarse_ids = lax.broadcasted_iota(jnp.int32, (coarse_count, mid_count), 0)
    selector = (coarse_ids == mid_parent[None, :]).astype(jnp.bfloat16)
    coarse_in = lax.psum(product(selector, mid_msg), ("rhombus", "tile"))
    coarse_out, down_coarse = coarse_update(
        coarse_latent, coarse_in, coarse_w1, coarse_w2, coarse_w3, w_descend
    )
    lookup = selector_rows(mid_parent, coarse_count)
    mid_out = (mid_up.astype(jnp.float32) + product(lookup, down_coarse)).astype(jnp.bfloat16)
    fine_down = product(mid_out, w_fine).astype(jnp.bfloat16)
    nearby = extended_2(fine_down, (("tile", 0),), mid_count)
    remapped = jnp.where(
        fine_parent < mid_count,
        fine_parent + mid_count,
        jnp.where(fine_parent < 2 * mid_count, fine_parent - mid_count, fine_parent),
    )
    parent_pick = selector_rows(remapped, 3 * mid_count)
    lifted = (fine_latent.astype(jnp.float32) + product(parent_pick, nearby)).astype(jnp.bfloat16)
    boundary = product(selector_rows(halo_rows, fine_count), lifted).astype(jnp.bfloat16)
    bordered = extended_2(boundary, (("tile", 0),), rim_count)
    node_table = jnp.concatenate([lifted, bordered[:rim_count], bordered[3 * rim_count :]], axis=0)
    fine_out = edge_update(
        node_table,
        lifted,
        edge_source,
        edge_target,
        edge_w_src,
        edge_w_dst,
        edge_w2,
        node_w1,
        node_w2,
        node_w3,
    )
    return (fine_out, mid_out, coarse_out)


def solution(mesh):
    placed = (
        P(("rhombus", "tile"), None),
        P(("rhombus", "tile"), None),
        P(),
        P(("rhombus", "tile")),
        P(("rhombus", "tile")),
        P(("rhombus", "tile")),
        P(("rhombus", "tile")),
        P(("rhombus", "tile")),
        P(),
        P(),
        P(),
        P(),
        P(),
        P(),
        P(),
        P(),
        P(),
        P(),
        P(),
        P(),
        P(),
        P(),
        P(),
        P(),
    )
    return jax.shard_map(
        on_device,
        mesh=mesh,
        in_specs=placed,
        out_specs=(P(("rhombus", "tile"), None), P(("rhombus", "tile"), None), P()),
        check_vma=False,
    )
```

profile of v0, /device:TPU:1, one launch (start us, length us, event | category | flops | bytes accessed | tf_op | source)
XLA Modules:
  0.0 112.6 jit_solution(14659364361576790947)
XLA Ops:
  0.7 1.9 %fusion.9 = f32[96,512]{1,0:T(8,128)S(1)} fusion(bf16[512,512]{1,0:T(8,128)(2,1)} %param.24, bf16[512,512]{1,0:T(8,128)(2,1)} %param.32, s32[512]{0:T(512)} %param.27), kind=kOutput, calls=%fused_computation.23 | convolution fusion | flops 319078400 | bytes 1247232 | tf_op jit(solution)/shard_map/dot_general | solution.py:23
  2.7 4.6 %collective-permute-start = (f32[32,512]{1,0:T(8,128)S(1)}, f32[32,512]{1,0:T(8,128)S(1)}, u32[]{:S(2)}, u32[]{:S(2)}) collective-permute-start(f32[32,512]{1,0:T(8,128)S(1)} %get-tuple-element.5), channel_id=1, source_target_pairs={{0,1},{1,2},{2,3},{3,4},{4,5},{5,6},{6,7},{8,9},{9,10},{10,11},{11... | collective-permute-start | bytes 196616 | tf_op jit(solution)/shard_map/ppermute | solution.py:16
  7.3 1.9 %collective-permute-start.1 = (f32[32,512]{1,0:T(8,128)S(1)}, f32[32,512]{1,0:T(8,128)S(1)}, u32[]{:S(2)}, u32[]{:S(2)}) collective-permute-start(f32[32,512]{1,0:T(8,128)S(1)} %get-tuple-element.6), channel_id=1, source_target_pairs={{1,0},{2,1},{3,2},{4,3},{5,4},{6,5},{7,6},{9,8},{10,9},{11,10},{12... | collective-permute-start | bytes 196616 | tf_op jit(solution)/shard_map/ppermute | solution.py:17
  9.2 1.6 %fusion.51 = f32[642,512]{1,0:T(8,128)} fusion(bf16[642,512]{1,0:T(8,128)(2,1)S(1)} %copy-done.1, bf16[512,512]{1,0:T(8,128)(2,1)S(1)} %copy-done.3), kind=kOutput, calls=%fused_computation.80 | convolution fusion | flops 336592896 | bytes 2496512 | tf_op jit(solution)/shard_map/dot_general | solution.py:23
  11.1 1.8 %collective-permute-done.1 = f32[32,512]{1,0:T(8,128)S(1)} collective-permute-done((f32[32,512]{1,0:T(8,128)S(1)}, f32[32,512]{1,0:T(8,128)S(1)}, u32[]{:S(2)}, u32[]{:S(2)}) %collective-permute-start.1) | collective-permute-done | bytes 65568 | tf_op jit(solution)/shard_map/ppermute | solution.py:17
  12.9 0.5 multiply_reduce_fusion.2
  13.5 0.5 fusion.12
  14.0 54.2 %all-reduce.1 = bf16[642,512]{1,0:T(8,128)(2,1)S(1)} all-reduce(f32[642,512]{1,0:T(8,128)S(1)} %fusion.12), channel_id=1, replica_groups=mesh['rhombus'=4,'tile'=8] {'rhombus','tile'}, use_global_device_ids=true, to_apply=%region_1.2 | all-reduce | flops 328704 | bytes 1972224 | tf_op jit(solution)/shard_map/psum | solution.py:102
  68.3 2.8 %multiply_reduce_fusion = (f32[642]{0:T(1024)S(1)}, f32[642,512]{1,0:T(8,128)S(1)}) fusion(bf16[512,512]{1,0:T(8,128)(2,1)} %param.39, f32[642,512]{1,0:T(8,128)} %fusion.51, bf16[512,512]{1,0:T(8,128)(2,1)} %param.38, bf16[642,512]{1,0:T(8,128)(2,1)S(1)} %all-reduce.1), kind=kOutput, calls=%fused_computation.15 | convolution fusion | flops 675814784 | bytes 4338184 | tf_op jit(solution)/shard_map/dot_general | solution.py:23
  71.4 2.0 %fusion.11 = bf16[32,512]{1,0:T(8,128)(2,1)S(1)} fusion(bf16[642,512]{1,0:T(8,128)(2,1)S(1)} %add_convert_fusion, bf16[512,512]{1,0:T(8,128)(2,1)} %param.40, bf16[32,512]{1,0:T(8,128)(2,1)S(1)} %add_convert_fusion.2, s32[32]{0:T(128)S(1)} %copy-done.14), kind=kOutput, calls=%fused_computation.27 | convolution fusion | flops 358028352 | bytes 1247360 | tf_op jit(solution)/shard_map/dot_general | solution.py:23
  73.5 4.6 %collective-permute-start.2 = (bf16[32,512]{1,0:T(8,128)(2,1)S(1)}, bf16[32,512]{1,0:T(8,128)(2,1)S(1)}, u32[]{:S(2)}, u32[]{:S(2)}) collective-permute-start(bf16[32,512]{1,0:T(8,128)(2,1)S(1)} %convolution_convert_fusion.6), channel_id=1, source_target_pairs={{0,1},{1,2},{2,3},{3,4},{4,5},{5,6},{6,7},{8,9},{9,10},{10,11},{11... | collective-permute-start | bytes 98312 | tf_op jit(solution)/shard_map/ppermute | solution.py:16
  78.1 1.9 %collective-permute-start.3 = (bf16[32,512]{1,0:T(8,128)(2,1)S(1)}, bf16[32,512]{1,0:T(8,128)(2,1)S(1)}, u32[]{:S(2)}, u32[]{:S(2)}) collective-permute-start(bf16[32,512]{1,0:T(8,128)(2,1)S(1)} %convolution_convert_fusion.6), channel_id=1, source_target_pairs={{1,0},{2,1},{3,2},{4,3},{5,4},{6,5},{7,6},{9,8},{10,9},{11,10},{12... | collective-permute-start | bytes 98312 | tf_op jit(solution)/shard_map/ppermute | solution.py:17
  80.1 3.3 %collective-permute-done.3 = bf16[32,512]{1,0:T(8,128)(2,1)S(1)} collective-permute-done((bf16[32,512]{1,0:T(8,128)(2,1)S(1)}, bf16[32,512]{1,0:T(8,128)(2,1)S(1)}, u32[]{:S(2)}, u32[]{:S(2)}) %collective-permute-start.3) | collective-permute-done | bytes 32800 | tf_op jit(solution)/shard_map/ppermute | solution.py:17
  83.4 0.4 fusion.6
  84.1 1.9 %collective-permute-start.4 = (bf16[128,512]{1,0:T(8,128)(2,1)S(1)}, bf16[128,512]{1,0:T(8,128)(2,1)}, u32[]{:S(2)}, u32[]{:S(2)}) collective-permute-start(bf16[128,512]{1,0:T(8,128)(2,1)S(1)} %get-tuple-element.3), channel_id=1, source_target_pairs={{0,1},{1,2},{2,3},{3,4},{4,5},{5,6},{6,7},{8,9},{9,10},{10,11},{11... | collective-permute-start | bytes 393224 | tf_op jit(solution)/shard_map/ppermute | solution.py:16
  86.1 3.3 %collective-permute-start.5 = (bf16[128,512]{1,0:T(8,128)(2,1)S(1)}, bf16[128,512]{1,0:T(8,128)(2,1)}, u32[]{:S(2)}, u32[]{:S(2)}) collective-permute-start(bf16[128,512]{1,0:T(8,128)(2,1)S(1)} %get-tuple-element.4), channel_id=1, source_target_pairs={{1,0},{2,1},{3,2},{4,3},{5,4},{6,5},{7,6},{9,8},{10,9},{11,10},{12... | collective-permute-start | bytes 393224 | tf_op jit(solution)/shard_map/ppermute | solution.py:17
  89.5 4.8 %fusion.2 = f32[3072,512]{1,0:T(8,128)} fusion(s32[3072]{0:T(1024)S(1)} %copy-done.16, bf16[512,512]{1,0:T(8,128)(2,1)S(1)} %fusion.6, bf16[512,512]{1,0:T(8,128)(2,1)S(1)} %copy-done), kind=kOutput, calls=%fused_computation.5 | convolution fusion | flops 1880883200 | bytes 7352320 | tf_op jit(solution)/shard_map/dot_general | solution.py:23
  94.3 0.4 fusion.52
  94.7 0.6 copy-done.15
  95.3 2.5 %convolution_convert_fusion = bf16[768,512]{1,0:T(8,128)(2,1)} fusion(bf16[512,512]{1,0:T(8,128)(2,1)S(1)} %copy-done.15, bf16[128,512]{1,0:T(8,128)(2,1)} %collective-permute-done.5, bf16[128,512]{1,0:T(8,128)(2,1)} %collective-permute-done.4, bf16[512,512]{1,0:T(8,128)(2,1)S(1)} %fusion.6), kind=kOutput, calls=%fused_computation.10 | convolution fusion | flops 405405696 | bytes 2097152 | tf_op jit(solution)/shard_map/dot_general | solution.py:23
  97.8 8.3 %fusion.1 = f32[512,512]{1,0:T(8,128)S(1)} fusion(s32[3072]{0:T(1024)S(1)} %copy-done.16, f32[3072,512]{1,0:T(8,128)} %fusion.2, bf16[768,512]{1,0:T(8,128)(2,1)} %convolution_convert_fusion, s32[3072]{0:T(1024)S(1)} %copy-done.17), kind=kOutput, calls=%fused_computation.4 | convolution fusion | flops 4039901184 | bytes 8151040 | tf_op jit(solution)/shard_map/dot_general | solution.py:55
  106.0 2.8 %convolution_convert_fusion.4 = bf16[512,512]{1,0:T(8,128)(2,1)} fusion(f32[512,512]{1,0:T(8,128)S(1)} %fusion.1, bf16[512,512]{1,0:T(8,128)(2,1)} %param.44), kind=kOutput, calls=%fused_computation.20 | convolution fusion | flops 1610874880 | bytes 2097152 | tf_op jit(solution)/shard_map/dot_general | solution.py:58
  108.9 2.4 %multiply_reduce_fusion.1 = (f32[512]{0:T(512)S(1)}, f32[512,512]{0,1:T(8,128)S(1)}) fusion(bf16[512,512]{1,0:T(8,128)(2,1)} %param.47, f32[512,512]{1,0:T(8,128)S(1)} %fusion.52, bf16[512,512]{1,0:T(8,128)(2,1)} %convolution_convert_fusion.4, bf16[512,512]{1,0:T(8,128)(2,1)} %param.46), kind=kOutput, calls=%fused_computation.32 | convolution fusion | flops 538967552 | bytes 3672064 | tf_op jit(solution)/shard_map/dot_general | solution.py:23
  111.6 1.0 add_convert_fusion.1
  (53 shorter events, 1.6 us)
Async XLA Ops:
  0.6 88.8 %copy-start = (bf16[512,512]{1,0:T(8,128)(2,1)S(1)}, bf16[512,512]{1,0:T(8,128)(2,1)}, u32[]{:S(2)}) copy-start(bf16[512,512]{1,0:T(8,128)(2,1)} %param.43) | copy-start | bytes 1572868
  0.6 8.6 %copy-start.1 = (bf16[642,512]{1,0:T(8,128)(2,1)S(1)}, bf16[642,512]{1,0:T(8,128)(2,1)}, u32[]{:S(2)}) copy-start(bf16[642,512]{1,0:T(8,128)(2,1)} %param.26) | copy-start | bytes 1972228
  0.7 8.6 %copy-start.3 = (bf16[512,512]{1,0:T(8,128)(2,1)S(1)}, bf16[512,512]{1,0:T(8,128)(2,1)}, u32[]{:S(2)}) copy-start(bf16[512,512]{1,0:T(8,128)(2,1)} %param.37) | copy-start | bytes 1572868
  2.6 8.3 %copy-start.6 = (bf16[512,512]{1,0:T(8,128)(2,1)S(1)}, bf16[512,512]{1,0:T(8,128)(2,1)}, u32[]{:S(2)}) copy-start(bf16[512,512]{1,0:T(8,128)(2,1)} %param.33) | copy-start | bytes 1572868
  2.6 8.2 %copy-start.11 = (bf16[32,512]{1,0:T(8,128)(2,1)S(1)}, bf16[32,512]{1,0:T(8,128)(2,1)}, u32[]{:S(2)}) copy-start(bf16[32,512]{1,0:T(8,128)(2,1)} %param.25) | copy-start | bytes 98308
  2.6 10.2 %copy-start.4 = (bf16[512,512]{1,0:T(8,128)(2,1)S(1)}, bf16[512,512]{1,0:T(8,128)(2,1)}, u32[]{:S(2)}) copy-start(bf16[512,512]{1,0:T(8,128)(2,1)} %param.35) | copy-start | bytes 1572868
  2.7 10.2 %copy-start.5 = (bf16[512,512]{1,0:T(8,128)(2,1)S(1)}, bf16[512,512]{1,0:T(8,128)(2,1)}, u32[]{:S(2)}) copy-start(bf16[512,512]{1,0:T(8,128)(2,1)} %param.34) | copy-start | bytes 1572868
  2.7 8.4 %collective-permute-start = (f32[32,512]{1,0:T(8,128)S(1)}, f32[32,512]{1,0:T(8,128)S(1)}, u32[]{:S(2)}, u32[]{:S(2)}) collective-permute-start(f32[32,512]{1,0:T(8,128)S(1)} %get-tuple-element.5), channel_id=1, source_target_pairs={{0,1},{1,2},{2,3},{3,4},{4,5},{5,6},{6,7},{8,9},{9,10},{10,11},{11... | collective-permute-start | bytes 196616 | tf_op jit(solution)/shard_map/ppermute | solution.py:16
  7.3 5.6 %collective-permute-start.1 = (f32[32,512]{1,0:T(8,128)S(1)}, f32[32,512]{1,0:T(8,128)S(1)}, u32[]{:S(2)}, u32[]{:S(2)}) collective-permute-start(f32[32,512]{1,0:T(8,128)S(1)} %get-tuple-element.6), channel_id=1, source_target_pairs={{1,0},{2,1},{3,2},{4,3},{5,4},{6,5},{7,6},{9,8},{10,9},{11,10},{12... | collective-permute-start | bytes 196616 | tf_op jit(solution)/shard_map/ppermute | solution.py:17
  10.9 2.6 %copy-start.9 = (bf16[512,512]{1,0:T(8,128)(2,1)S(1)}, bf16[512,512]{1,0:T(8,128)(2,1)}, u32[]{:S(2)}) copy-start(bf16[512,512]{1,0:T(8,128)(2,1)} %param.36) | copy-start | bytes 1572868
  10.9 2.6 %copy-start.14 = (s32[32]{0:T(128)S(1)}, s32[32]{0:T(128)}, u32[]{:S(2)}) copy-start(s32[32]{0:T(128)} %param.28) | copy-start | bytes 388
  71.3 12.4 %copy-start.2 = (bf16[642,512]{1,0:T(8,128)(2,1)}, bf16[642,512]{1,0:T(8,128)(2,1)S(1)}, u32[]{:S(2)}) copy-start(bf16[642,512]{1,0:T(8,128)(2,1)S(1)} %add_convert_fusion) | copy-start | bytes 1972228
  71.3 2.0 %copy-start.7 = (bf16[512,512]{1,0:T(8,128)(2,1)S(1)}, bf16[512,512]{1,0:T(8,128)(2,1)}, u32[]{:S(2)}) copy-start(bf16[512,512]{1,0:T(8,128)(2,1)} %param.41) | copy-start | bytes 1572868
  71.3 8.8 %copy-start.13 = (s32[512]{0:T(512)S(1)}, s32[512]{0:T(512)}, u32[]{:S(2)}) copy-start(s32[512]{0:T(512)} %param.27) | copy-start | bytes 6148
  71.3 12.0 %copy-start.8 = (bf16[512,512]{1,0:T(8,128)(2,1)S(1)}, bf16[512,512]{1,0:T(8,128)(2,1)}, u32[]{:S(2)}) copy-start(bf16[512,512]{1,0:T(8,128)(2,1)} %param.24) | copy-start | bytes 1572868
  71.3 12.4 %copy-start.18 = (s32[256]{0:T(256)S(1)}, s32[256]{0:T(256)}, u32[]{:S(2)}) copy-start(s32[256]{0:T(256)} %param.29) | copy-start | bytes 3076
  73.3 20.9 %copy-start.12 = (bf16[32,512]{1,0:T(8,128)(2,1)}, bf16[32,512]{1,0:T(8,128)(2,1)S(1)}, u32[]{:S(2)}) copy-start(bf16[32,512]{1,0:T(8,128)(2,1)S(1)} %fusion.11) | copy-start | bytes 98308
  73.3 16.1 %copy-start.16 = (s32[3072]{0:T(1024)S(1)}, s32[3072]{0:T(1024)}, u32[]{:S(2)}) copy-start(s32[3072]{0:T(1024)} %param.31) | copy-start | bytes 36868
  73.5 6.6 %collective-permute-start.2 = (bf16[32,512]{1,0:T(8,128)(2,1)S(1)}, bf16[32,512]{1,0:T(8,128)(2,1)S(1)}, u32[]{:S(2)}, u32[]{:S(2)}) collective-permute-start(bf16[32,512]{1,0:T(8,128)(2,1)S(1)} %convolution_convert_fusion.6), channel_id=1, source_target_pairs={{0,1},{1,2},{2,3},{3,4},{4,5},{5,6},{6,7},{8,9},{9,10},{10,11},{11... | collective-permute-start | bytes 98312 | tf_op jit(solution)/shard_map/ppermute | solution.py:16
  78.1 5.2 %collective-permute-start.3 = (bf16[32,512]{1,0:T(8,128)(2,1)S(1)}, bf16[32,512]{1,0:T(8,128)(2,1)S(1)}, u32[]{:S(2)}, u32[]{:S(2)}) collective-permute-start(bf16[32,512]{1,0:T(8,128)(2,1)S(1)} %convolution_convert_fusion.6), channel_id=1, source_target_pairs={{1,0},{2,1},{3,2},{4,3},{5,4},{6,5},{7,6},{9,8},{10,9},{11,10},{12... | collective-permute-start | bytes 98312 | tf_op jit(solution)/shard_map/ppermute | solution.py:17
  84.1 10.6 %collective-permute-start.4 = (bf16[128,512]{1,0:T(8,128)(2,1)S(1)}, bf16[128,512]{1,0:T(8,128)(2,1)}, u32[]{:S(2)}, u32[]{:S(2)}) collective-permute-start(bf16[128,512]{1,0:T(8,128)(2,1)S(1)} %get-tuple-element.3), channel_id=1, source_target_pairs={{0,1},{1,2},{2,3},{3,4},{4,5},{5,6},{6,7},{8,9},{9,10},{10,11},{11... | collective-permute-start | bytes 393224 | tf_op jit(solution)/shard_map/ppermute | solution.py:16
  86.1 8.2 %copy-start.10 = (bf16[512,512]{1,0:T(8,128)(2,1)S(1)}, bf16[512,512]{1,0:T(8,128)(2,1)}, u32[]{:S(2)}) copy-start(bf16[512,512]{1,0:T(8,128)(2,1)} %param.45) | copy-start | bytes 1572868
  86.1 8.6 %collective-permute-start.5 = (bf16[128,512]{1,0:T(8,128)(2,1)S(1)}, bf16[128,512]{1,0:T(8,128)(2,1)}, u32[]{:S(2)}, u32[]{:S(2)}) collective-permute-start(bf16[128,512]{1,0:T(8,128)(2,1)S(1)} %get-tuple-element.4), channel_id=1, source_target_pairs={{1,0},{2,1},{3,2},{4,3},{5,4},{6,5},{7,6},{9,8},{10,9},{11,10},{12... | collective-permute-start | bytes 393224 | tf_op jit(solution)/shard_map/ppermute | solution.py:17
  94.7 3.1 %copy-start.17 = (s32[3072]{0:T(1024)S(1)}, s32[3072]{0:T(1024)}, u32[]{:S(2)}) copy-start(s32[3072]{0:T(1024)} %param.30) | copy-start | bytes 36868
  (1 other events, 1.0 us)
where the time goes:
time: 113 us
  blocking collectives  54.2 us (48%)
  matrix products  31.5 us (28%)
  starting transfers between devices  18.3 us (16%)
  waiting for transfers between devices  5.11 us (5%)
  other arithmetic  1.4 us (1%)
    psum x1, blocking collectives, on_device(): coarse_in = lax.psum(product(selector, mid_msg), ('rhombus', 'tile'))  54.2 us
    dot_general x14, matrix products, product(): return jnp.dot(left, right, preferred_element_type=jnp.float32)  20.4 us
    ppermute x3, starting transfers between devices, extended_2(): before = lax.ppermute(last, axis, up)  11.1 us
    dot_general x1, matrix products, edge_update(): lax.dot_general(target_pick, edge_hidden, (((0,), (0,)), ((), ())), prefe...  8.28 us
    ppermute x3, starting transfers between devices, extended_2(): after = lax.ppermute(leading, axis, down)  7.19 us
    ppermute x3, waiting for transfers between devices, extended_2(): after = lax.ppermute(leading, axis, down)  5.11 us
    dot_general x1, matrix products, edge_update(): jnp.dot(hidden_sums, edge_w2.astype(jnp.float32), precision=lax.Precision...  2.83 us
  transfers between devices with their start and end apart: 6, of which 2 were waited for; matrix products, arithmetic and copies ran while one was open for 6% of the time, Pallas kernels for 0%

commit v1 on v0

--- a/solution.py
+++ b/solution.py
@@ -99,7 +99,7 @@
     mid_msg = product(mid_up, w_coarse).astype(jnp.bfloat16)
     coarse_ids = lax.broadcasted_iota(jnp.int32, (coarse_count, mid_count), 0)
     selector = (coarse_ids == mid_parent[None, :]).astype(jnp.bfloat16)
-    coarse_in = lax.psum(product(selector, mid_msg), ("rhombus", "tile"))
+    coarse_in = jnp.sum(lax.all_gather(product(selector, mid_msg), ("rhombus", "tile")), axis=0)
     coarse_out, down_coarse = coarse_update(
         coarse_latent, coarse_in, coarse_w1, coarse_w2, coarse_w3, w_descend
     )

time: 113 us -> 327 us (2.89)
  waiting for transfers between devices: 5.11 us -> 244 us
  blocking collectives: 54.2 us -> 0 us
  other arithmetic: 1.4 us -> 19.6 us
  between operations: 1.03 us -> 14.4 us
    all_gather x0 -> x1, waiting for transfers between devices: none -> 238 us  [on_device(): lax.all_gather(product(selector, mid_msg), ('rhombus', 'tile'))]
    psum x1 -> x0, blocking collectives: 54.2 us -> none  [on_device(): coarse_in = lax.psum(product(selector, mid_msg), ('rhombus', 'tile'))]
    reduce_sum x0 -> x1, other arithmetic: none -> 16.8 us  [on_device(): jnp.sum(lax.all_gather(product(selector, mid_msg), ('rhombus', 'tile')),...]
  transfers between devices with their start and end apart: 6 -> 7, of which waited for: 2 -> 3; matrix products, arithmetic and copies ran while one was open for 6% -> 2% of each run, Pallas kernels for 0% -> 0%
where the time goes in v1:
time: 327 us; the launch traced here: 326 us
  waiting for transfers between devices  244 us (75%)
  matrix products  29.9 us (9%)
  other arithmetic  19.6 us (6%)
  starting transfers between devices  16.2 us (5%)
  between operations  14.4 us (4%)
    all_gather x1, waiting for transfers between devices, on_device(): lax.all_gather(product(selector, mid_msg), ('rhombus', 'tile'))  238 us
    dot_general x14, matrix products, product(): return jnp.dot(left, right, preferred_element_type=jnp.float32)  19.8 us
    reduce_sum x1, other arithmetic, on_device(): jnp.sum(lax.all_gather(product(selector, mid_msg), ('rhombus', 'tile')),...  16.8 us
    ppermute x3, starting transfers between devices, extended_2(): before = lax.ppermute(last, axis, up)  9.62 us
    dot_general x1, matrix products, edge_update(): lax.dot_general(target_pick, edge_hidden, (((0,), (0,)), ((), ())), prefe...  8.33 us
    ppermute x3, waiting for transfers between devices, extended_2(): after = lax.ppermute(leading, axis, down)  6.72 us
    ppermute x3, starting transfers between devices, extended_2(): after = lax.ppermute(leading, axis, down)  6.56 us
  transfers between devices with their start and end apart: 7, of which 3 were waited for; matrix products, arithmetic and copies ran while one was open for 2% of the time, Pallas kernels for 0%

profile of v1, /device:TPU:1, one launch (start us, length us, event | category | flops | bytes accessed | tf_op | source)
XLA Modules:
  0.0 326.2 jit_solution(4855994777211288693)
XLA Ops:
  7.3 1.9 fusion.9
  9.2 4.5 %collective-permute-start = (f32[32,512]{1,0:T(8,128)S(1)}, f32[32,512]{1,0:T(8,128)S(1)}, u32[]{:S(2)}, u32[]{:S(2)}) collective-permute-start(f32[32,512]{1,0:T(8,128)S(1)} %get-tuple-element.5), channel_id=1, source_target_pairs={{0,1},{1,2},{2,3},{3,4},{4,5},{5,6},{6,7},{8,9},{9,10},{10,11},{11... | collective-permute-start | bytes 196616 | tf_op jit(solution)/shard_map/ppermute | solution.py:16
  13.7 1.9 collective-permute-start.1
  15.9 3.4 %collective-permute-done.1 = f32[32,512]{1,0:T(8,128)S(1)} collective-permute-done((f32[32,512]{1,0:T(8,128)S(1)}, f32[32,512]{1,0:T(8,128)S(1)}, u32[]{:S(2)}, u32[]{:S(2)}) %collective-permute-start.1) | collective-permute-done | bytes 65568 | tf_op jit(solution)/shard_map/ppermute | solution.py:17
  20.0 2.8 convolution_bitcast_fusion
  22.8 0.5 fusion.50
  23.3 237.7 %all-gather.4.cloned.1.call-done = f32[32,642,512]{2,1,0:T(8,128)} async-done(((f32[1,642,512]{2,1,0:T(8,128)}), f32[32,642,512]{2,1,0:T(8,128)}) %all-gather.4.cloned.1.call-update) | async-done | bytes 42074128 | tf_op jit(solution)/shard_map/all_gather | solution.py:102
  261.0 16.8 %reduce_sum.37 = bf16[642,512]{1,0:T(8,128)(2,1)S(1)} reduce(f32[32,642,512]{2,1,0:T(8,128)} %all-gather.4.cloned.1.call-done, f32[]{:T(128)} %constant.15.clone.1), dimensions={0}, to_apply=%region_1.2 | reduce | flops 10189824 | bytes 42731524 | tf_op jit(solution)/shard_map/reduce_sum | solution.py:102
  277.8 3.3 %multiply_reduce_fusion = (f32[642]{0:T(1024)S(1)}, f32[642,512]{1,0:T(8,128)}) fusion(bf16[512,512]{1,0:T(8,128)(2,1)} %param.39, f32[642,512]{1,0:T(8,128)S(1)} %fusion.50, bf16[512,512]{1,0:T(8,128)(2,1)} %param.38, bf16[642,512]{1,0:T(8,128)(2,1)S(1)} %reduce_sum.37), kind=kOutput, calls=%fused_computation.16 | convolution fusion | flops 675814784 | bytes 4338184 | tf_op jit(solution)/shard_map/dot_general | solution.py:23
  281.1 1.6 add_convert_fusion
  282.9 0.6 fusion.11
  283.5 0.6 copy-done.8
  284.3 3.2 collective-permute-start.2
  287.5 1.9 collective-permute-start.3
  289.5 3.3 %collective-permute-done.3 = bf16[32,512]{1,0:T(8,128)(2,1)S(1)} collective-permute-done((bf16[32,512]{1,0:T(8,128)(2,1)S(1)}, bf16[32,512]{1,0:T(8,128)(2,1)S(1)}, u32[]{:S(2)}, u32[]{:S(2)}) %collective-permute-start.3) | collective-permute-done | bytes 32800 | tf_op jit(solution)/shard_map/ppermute | solution.py:17
  293.5 1.9 collective-permute-start.4
  295.4 2.7 collective-permute-start.5
  298.2 4.8 %fusion.2 = f32[3072,512]{1,0:T(8,128)} fusion(s32[3072]{0:T(1024)S(1)} %copy-done.18, bf16[512,512]{1,0:T(8,128)(2,1)S(1)} %fusion.6, bf16[512,512]{1,0:T(8,128)(2,1)S(1)} %copy-done), kind=kOutput, calls=%fused_computation.5 | convolution fusion | flops 1880883200 | bytes 7352320 | tf_op jit(solution)/shard_map/dot_general | solution.py:23
  303.5 0.6 copy-done.17
  304.0 1.5 convolution_convert_fusion
  305.5 8.3 %fusion.1 = f32[512,512]{1,0:T(8,128)S(1)} fusion(s32[3072]{0:T(1024)S(1)} %copy-done.18, f32[3072,512]{1,0:T(8,128)} %fusion.2, bf16[768,512]{1,0:T(8,128)(2,1)} %convolution_convert_fusion, s32[3072]{0:T(1024)S(1)} %copy-done.19), kind=kOutput, calls=%fused_computation.4 | convolution fusion | flops 4039901184 | bytes 8151040 | tf_op jit(solution)/shard_map/dot_general | solution.py:55
  313.8 1.8 convolution_convert_fusion.4
  315.6 2.4 multiply_reduce_fusion.1
  318.4 1.0 add_convert_fusion.1
  (60 shorter events, 2.6 us)
Async XLA Ops:
  7.2 291.0 %copy-start = (bf16[512,512]{1,0:T(8,128)(2,1)S(1)}, bf16[512,512]{1,0:T(8,128)(2,1)}, u32[]{:S(2)}) copy-start(bf16[512,512]{1,0:T(8,128)(2,1)} %param.43) | copy-start | bytes 1572868
  7.2 8.5 %copy-start.12 = (bf16[32,512]{1,0:T(8,128)(2,1)S(1)}, bf16[32,512]{1,0:T(8,128)(2,1)}, u32[]{:S(2)}) copy-start(bf16[32,512]{1,0:T(8,128)(2,1)} %param.25) | copy-start | bytes 98308
  7.2 8.5 %copy-start.7 = (bf16[512,512]{1,0:T(8,128)(2,1)S(1)}, bf16[512,512]{1,0:T(8,128)(2,1)}, u32[]{:S(2)}) copy-start(bf16[512,512]{1,0:T(8,128)(2,1)} %param.33) | copy-start | bytes 1572868
  7.2 12.1 %copy-start.5 = (bf16[512,512]{1,0:T(8,128)(2,1)S(1)}, bf16[512,512]{1,0:T(8,128)(2,1)}, u32[]{:S(2)}) copy-start(bf16[512,512]{1,0:T(8,128)(2,1)} %param.34) | copy-start | bytes 1572868
  7.2 12.1 %copy-start.4 = (bf16[512,512]{1,0:T(8,128)(2,1)S(1)}, bf16[512,512]{1,0:T(8,128)(2,1)}, u32[]{:S(2)}) copy-start(bf16[512,512]{1,0:T(8,128)(2,1)} %param.35) | copy-start | bytes 1572868
  7.2 253.7 %all-gather.4.cloned.1.call-start = ((), (), s32[]{:S(2)}) async-start(), calls=%async_computation | async-start | bytes 43794432 | tf_op jit(solution)/shard_map/all_gather | solution.py:102
  9.2 10.7 %copy-start.15 = (s32[32]{0:T(128)S(1)}, s32[32]{0:T(128)}, u32[]{:S(2)}) copy-start(s32[32]{0:T(128)} %param.28) | copy-start | bytes 388
  9.2 6.6 %collective-permute-start = (f32[32,512]{1,0:T(8,128)S(1)}, f32[32,512]{1,0:T(8,128)S(1)}, u32[]{:S(2)}, u32[]{:S(2)}) collective-permute-start(f32[32,512]{1,0:T(8,128)S(1)} %get-tuple-element.5), channel_id=1, source_target_pairs={{0,1},{1,2},{2,3},{3,4},{4,5},{5,6},{6,7},{8,9},{9,10},{10,11},{11... | collective-permute-start | bytes 196616 | tf_op jit(solution)/shard_map/ppermute | solution.py:16
  13.7 5.6 %collective-permute-start.1 = (f32[32,512]{1,0:T(8,128)S(1)}, f32[32,512]{1,0:T(8,128)S(1)}, u32[]{:S(2)}, u32[]{:S(2)}) collective-permute-start(f32[32,512]{1,0:T(8,128)S(1)} %get-tuple-element.6), channel_id=1, source_target_pairs={{1,0},{2,1},{3,2},{4,3},{5,4},{6,5},{7,6},{9,8},{10,9},{11,10},{12... | collective-permute-start | bytes 196616 | tf_op jit(solution)/shard_map/ppermute | solution.py:17
  19.9 2.8 copy-start.2
  20.0 2.8 copy-start.6
  282.8 10.3 %copy-start.3 = (bf16[642,512]{1,0:T(8,128)(2,1)}, bf16[642,512]{1,0:T(8,128)(2,1)S(1)}, u32[]{:S(2)}) copy-start(bf16[642,512]{1,0:T(8,128)(2,1)S(1)} %add_convert_fusion) | copy-start | bytes 1972228
  282.8 6.6 %copy-start.14 = (s32[512]{0:T(512)S(1)}, s32[512]{0:T(512)}, u32[]{:S(2)}) copy-start(s32[512]{0:T(512)} %param.27) | copy-start | bytes 6148
  282.9 9.9 %copy-start.9 = (bf16[512,512]{1,0:T(8,128)(2,1)S(1)}, bf16[512,512]{1,0:T(8,128)(2,1)}, u32[]{:S(2)}) copy-start(bf16[512,512]{1,0:T(8,128)(2,1)} %param.24) | copy-start | bytes 1572868
  282.9 10.2 %copy-start.20 = (s32[256]{0:T(256)S(1)}, s32[256]{0:T(256)}, u32[]{:S(2)}) copy-start(s32[256]{0:T(256)} %param.29) | copy-start | bytes 3076
  284.1 18.9 %copy-start.13 = (bf16[32,512]{1,0:T(8,128)(2,1)}, bf16[32,512]{1,0:T(8,128)(2,1)S(1)}, u32[]{:S(2)}) copy-start(bf16[32,512]{1,0:T(8,128)(2,1)S(1)} %fusion.11) | copy-start | bytes 98308
  284.1 14.1 %copy-start.18 = (s32[3072]{0:T(1024)S(1)}, s32[3072]{0:T(1024)}, u32[]{:S(2)}) copy-start(s32[3072]{0:T(1024)} %param.31) | copy-start | bytes 36868
  284.3 5.2 %collective-permute-start.2 = (bf16[32,512]{1,0:T(8,128)(2,1)S(1)}, bf16[32,512]{1,0:T(8,128)(2,1)S(1)}, u32[]{:S(2)}, u32[]{:S(2)}) collective-permute-start(bf16[32,512]{1,0:T(8,128)(2,1)S(1)} %convolution_convert_fusion.6), channel_id=1, source_target_pairs={{0,1},{1,2},{2,3},{3,4},{4,5},{5,6},{6,7},{8,9},{9,10},{10,11},{11... | collective-permute-start | bytes 98312 | tf_op jit(solution)/shard_map/ppermute | solution.py:16
  287.5 5.2 %collective-permute-start.3 = (bf16[32,512]{1,0:T(8,128)(2,1)S(1)}, bf16[32,512]{1,0:T(8,128)(2,1)S(1)}, u32[]{:S(2)}, u32[]{:S(2)}) collective-permute-start(bf16[32,512]{1,0:T(8,128)(2,1)S(1)} %convolution_convert_fusion.6), channel_id=1, source_target_pairs={{1,0},{2,1},{3,2},{4,3},{5,4},{6,5},{7,6},{9,8},{10,9},{11,10},{12... | collective-permute-start | bytes 98312 | tf_op jit(solution)/shard_map/ppermute | solution.py:17
  293.5 9.9 %collective-permute-start.4 = (bf16[128,512]{1,0:T(8,128)(2,1)S(1)}, bf16[128,512]{1,0:T(8,128)(2,1)S(1)}, u32[]{:S(2)}, u32[]{:S(2)}) collective-permute-start(bf16[128,512]{1,0:T(8,128)(2,1)S(1)} %get-tuple-element.3), channel_id=1, source_target_pairs={{0,1},{1,2},{2,3},{3,4},{4,5},{5,6},{6,7},{8,9},{9,10},{10,11},{11... | collective-permute-start | bytes 393224 | tf_op jit(solution)/shard_map/ppermute | solution.py:16
  295.4 7.5 %copy-start.10 = (bf16[512,512]{1,0:T(8,128)(2,1)S(1)}, bf16[512,512]{1,0:T(8,128)(2,1)}, u32[]{:S(2)}) copy-start(bf16[512,512]{1,0:T(8,128)(2,1)} %param.45) | copy-start | bytes 1572868
  295.4 8.0 %collective-permute-start.5 = (bf16[128,512]{1,0:T(8,128)(2,1)S(1)}, bf16[128,512]{1,0:T(8,128)(2,1)S(1)}, u32[]{:S(2)}, u32[]{:S(2)}) collective-permute-start(bf16[128,512]{1,0:T(8,128)(2,1)S(1)} %get-tuple-element.4), channel_id=1, source_target_pairs={{1,0},{2,1},{3,2},{4,3},{5,4},{6,5},{7,6},{9,8},{10,9},{11,10},{12... | collective-permute-start | bytes 393224 | tf_op jit(solution)/shard_map/ppermute | solution.py:17
  303.4 2.1 copy-start.19
  305.5 8.3 %copy-start.11 = (bf16[512,512]{1,0:T(8,128)(2,1)S(1)}, bf16[512,512]{1,0:T(8,128)(2,1)}, u32[]{:S(2)}) copy-start(bf16[512,512]{1,0:T(8,128)(2,1)} %param.44) | copy-start | bytes 1572868
  (4 other events, 5.4 us)
Sparse Core Ops, SparseCore 0:
  22.9 238.0 all-gather.3
